TPU v7x, 256 devices: a whole 4x4x8 slice. The times are simulated.
256 devices in a mesh: seq: 32 (over z, y), exp: 4 (over x), dp: 2 (over core).
Axes of the slice: x: 4, y: 4, z: 8, core: 2. Of those that a mesh axis runs over, the one named last changes fastest.
Arguments:
- head_inputs: bfloat16 [16384, 4096], P(('dp', 'seq'), 'exp'), parts along dimension 0, may hold values from -6 to 6
- input_matrix: bfloat16 [16384, 128], P(('dp', 'seq')), parts along dimension 0, may hold values from -0.015625 to 0.015625
- output_matrix: bfloat16 [16384, 128], P(('dp', 'seq')), parts along dimension 0, may hold values from -6 to 6
- log_decay: float32 [64, 16384], P('exp', ('dp', 'seq')), parts along dimension 1, may hold values from -1 to 0
- skip_gain: float32 [64], P('exp'), may hold values from 0.5 to 1.5
- residual: bfloat16 [16384, 4096], P(('dp', 'seq', 'exp')), parts along dimension 0, may hold values from -6 to 6
- norm_gain: float32 [4096], replicated, may hold values from 0.1 to 1.9
- router_weight: bfloat16 [4096, 16], replicated, may hold values from -0.09375 to 0.09375
- expert_ids: int32 [16384, 2], P(('dp', 'seq', 'exp')), parts along dimension 0, may hold values from 0 to 15, as said below
- gate_weight: bfloat16 [4, 4096, 12288], P('exp', None, 'seq'), may hold values from -0.09375 to 0.09375
- up_weight: bfloat16 [4, 4096, 12288], P('exp', None, 'seq'), may hold values from -0.09375 to 0.09375
- down_weight: bfloat16 [4, 12288, 4096], P('exp', 'seq'), may hold values from -0.0546875 to 0.0546875
Outputs:
- layer_out: bfloat16 [16384, 4096], P(('dp', 'seq', 'exp')), parts along dimension 0
There are 2 independent parts, one for each index of `dp`. A program takes and returns all parts, laid end to end along the dimension named above; an argument that names none is the same for every part. Nothing has to cross between parts.
Inputs may be any that keep to these rules, and one draw needn't show every extreme that they name: `expert_ids`: each row names two different experts; the second column never names an expert below 4. In every aligned block of 64 rows each expert below 4 is named by at most 8 rows, and in every run of 4 consecutive blocks, starting at block 0, by at most 16 rows; in every run one such expert is named by exactly 8 rows in one block and by exactly 16 rows in the whole run.
All inputs are finite; a program needn't handle non-finite values.
Results may differ from a plain program's by a relative error of at most 0.015.
Values may be sent and summed in bfloat16 or wider, within the bound.
A program may use at most 128 MiB of HBM per device.

v0:
```python
import jax
import jax.numpy as jnp
from jax import lax
from jax.sharding import PartitionSpec as P

P_SIZE = 64
CAP = 8


def shifted(block, axis, distance):
    devices = range(lax.axis_size(axis))
    route = [(i - distance, i) for i in devices if i - distance in devices]
    return lax.ppermute(block, axis, route)


def body(
    head_inputs,
    input_matrix,
    output_matrix,
    log_decay,
    skip_gain,
    residual,
    norm_gain,
    router_weight,
    expert_ids,
    gate_weight,
    up_weight,
    down_weight,
):
    length = head_inputs.shape[0]
    heads = log_decay.shape[0]
    per_head = head_inputs.reshape(length, heads, P_SIZE)
    cumulative = jnp.cumsum(log_decay, axis=1)
    scores = jnp.dot(output_matrix, input_matrix.T, preferred_element_type=jnp.float32)
    causal = lax.broadcasted_iota(jnp.int32, (length, length), 0) >= lax.broadcasted_iota(
        jnp.int32, (length, length), 1
    )
    spread = jnp.minimum(cumulative[:, :, None] - cumulative[:, None, :], 0.0)
    mixing = jnp.where(causal[None], jnp.exp(spread) * scores[None], 0.0).astype(jnp.bfloat16)
    within = jnp.einsum("hts,shp->thp", mixing, per_head, preferred_element_type=jnp.float32)
    remain = jnp.exp(cumulative[:, -1:] - cumulative)
    weighted = (remain[:, :, None] * input_matrix.astype(jnp.float32)[None]).astype(jnp.bfloat16)
    local_state = jnp.einsum("shp,hsn->hpn", per_head, weighted, preferred_element_type=jnp.float32)
    block_decay = jnp.exp(cumulative[:, -1])

    def advance(iteration, incoming):
        outgoing = block_decay[:, None, None] * incoming + local_state
        return shifted(outgoing.astype(jnp.bfloat16), "seq", 1).astype(outgoing.dtype)

    entering = lax.fori_loop(0, lax.axis_size("seq") - 1, advance, jnp.zeros_like(local_state))
    carried = jnp.einsum(
        "tn,hpn->thp", output_matrix.astype(jnp.float32), entering, precision=lax.Precision.HIGHEST
    )
    carried = carried * jnp.exp(cumulative).T[:, :, None]
    mixed = within + carried + skip_gain[None, :, None] * per_head.astype(jnp.float32)
    mamba_out = mixed.reshape(length, heads * P_SIZE).astype(jnp.bfloat16)
    token_rows = lax.all_to_all(mamba_out, "exp", split_axis=0, concat_axis=1, tiled=True)
    stream = (residual.astype(jnp.float32) + token_rows.astype(jnp.float32)).astype(jnp.bfloat16)
    stream_wide = stream.astype(jnp.float32)
    normed = (
        stream_wide
        * lax.rsqrt(jnp.mean(stream_wide * stream_wide, axis=-1, keepdims=True) + 1e-06)
        * norm_gain
    ).astype(jnp.bfloat16)
    logits = jnp.dot(normed, router_weight, preferred_element_type=jnp.float32)
    expert_iota = lax.broadcasted_iota(jnp.int32, logits.shape, 1)
    first = expert_ids[:, 0]
    second = expert_ids[:, 1]
    first_logit = jnp.sum(jnp.where(expert_iota == first[:, None], logits, 0.0), axis=-1)
    second_logit = jnp.sum(jnp.where(expert_iota == second[:, None], logits, 0.0), axis=-1)
    gate = jax.nn.sigmoid(first_logit - second_logit)
    flight = lax.axis_size("exp")
    member = (first[:, None] == jnp.arange(flight, dtype=jnp.int32)[None, :]).astype(jnp.int32)
    ranking = jnp.cumsum(member, axis=0) - member
    slots = jnp.sum(ranking * member, axis=-1)
    chosen = (member.T[:, None, :] == 1) & (
        slots[None, None, :] == jnp.arange(CAP, dtype=jnp.int32)[None, :, None]
    )
    select = chosen.astype(jnp.bfloat16)
    outbound = jnp.einsum("ecr,rd->ecd", select, normed, preferred_element_type=jnp.float32).astype(
        jnp.bfloat16
    )
    model_width = outbound.shape[2]
    inbound = lax.all_to_all(outbound, "exp", split_axis=0, concat_axis=0, tiled=True)
    routed = inbound.reshape(flight * CAP, model_width)
    gate_part = gate_weight[0]
    up_part = up_weight[0]
    down_part = down_weight[0]
    fragment = lax.all_gather(routed, "seq", axis=0, tiled=True)
    gated = jnp.dot(fragment, gate_part, preferred_element_type=jnp.float32)
    lifted = jnp.dot(fragment, up_part, preferred_element_type=jnp.float32)
    hidden_all = (jax.nn.silu(gated) * lifted).astype(jnp.bfloat16)
    fragment = hidden_all
    summed = lax.psum_scatter(
        jnp.dot(fragment, down_part, preferred_element_type=jnp.float32).astype(jnp.bfloat16),
        "seq",
        scatter_dimension=0,
        tiled=True,
    )
    expert_out = summed.reshape(flight, CAP, model_width)
    returned = lax.all_to_all(expert_out, "exp", split_axis=0, concat_axis=0, tiled=True)
    combined = jnp.einsum("ecr,ecd->rd", select, returned, preferred_element_type=jnp.float32)
    return (stream_wide + gate[:, None] * combined).astype(jnp.bfloat16)


def solution(mesh):
    return jax.shard_map(
        body,
        mesh=mesh,
        in_specs=(
            P(("dp", "seq"), "exp"),
            P(("dp", "seq"), None),
            P(("dp", "seq"), None),
            P("exp", ("dp", "seq")),
            P("exp"),
            P(("dp", "seq", "exp"), None),
            P(),
            P(),
            P(("dp", "seq", "exp"), None),
            P("exp", None, "seq"),
            P("exp", None, "seq"),
            P("exp", "seq", None),
        ),
        out_specs=P(("dp", "seq", "exp"), None),
        check_vma=False,
    )
```

profile of v0, /device:TPU:64, one launch (start us, length us, event | category | flops | bytes accessed | tf_op | source)
XLA Modules:
  0.0 889.1 jit_solution(8230713345053279905)
XLA Ops:
  20.3 442.0 %while.11 = (s32[]{:T(128)}, f32[16,64,128]{2,1,0:T(8,128)}, f32[16]{0:T(128)S(1)}, f32[16,64,128]{2,1,0:T(8,128)}, s32[]{:T(128)}, /*index=5*/s32[]{:T(128)}) while((s32[]{:T(128)}, f32[16,64,128]{2,1,0:T(8,128)}, f32[16]{0:T(128)S(1)}, f32[16,64,128]{2,1,0:T(8,128)}, s32[]{:T(128)}, /*index=5*/s32[]{:T(128)}) %tuple.33), condition=%wide.region_3.4_spmd.clone, body=%wide.region_2.3_spmd.clone.sunk | while | flops 655363 | bytes 3145911 | solution.py:50
  25.7 8.8 collective-permute-done
  39.3 9.5 %collective-permute-done = bf16[16,64,128]{2,1,0:T(8,128)(2,1)S(1)} collective-permute-done((bf16[16,64,128]{2,1,0:T(8,128)(2,1)}, bf16[16,64,128]{2,1,0:T(8,128)(2,1)S(1)}, u32[]{:S(2)}, u32[]{:S(2)}) %collective-permute-start) | collective-permute-done | bytes 262176 | tf_op jit(solution)/shard_map/while/body/eval_jaxpr/ppermute | solution.py:13
  53.6 8.7 collective-permute-done
  67.1 8.7 collective-permute-done
  80.6 8.7 collective-permute-done
  94.0 8.7 collective-permute-done
  107.5 8.7 collective-permute-done
  121.0 8.7 collective-permute-done
  134.5 8.9 collective-permute-done
  148.2 10.0 %collective-permute-done = bf16[16,64,128]{2,1,0:T(8,128)(2,1)S(1)} collective-permute-done((bf16[16,64,128]{2,1,0:T(8,128)(2,1)}, bf16[16,64,128]{2,1,0:T(8,128)(2,1)S(1)}, u32[]{:S(2)}, u32[]{:S(2)}) %collective-permute-start) | collective-permute-done | bytes 262176 | tf_op jit(solution)/shard_map/while/body/eval_jaxpr/ppermute | solution.py:13
  163.1 11.2 %collective-permute-done = bf16[16,64,128]{2,1,0:T(8,128)(2,1)S(1)} collective-permute-done((bf16[16,64,128]{2,1,0:T(8,128)(2,1)}, bf16[16,64,128]{2,1,0:T(8,128)(2,1)S(1)}, u32[]{:S(2)}, u32[]{:S(2)}) %collective-permute-start) | collective-permute-done | bytes 262176 | tf_op jit(solution)/shard_map/while/body/eval_jaxpr/ppermute | solution.py:13
  179.0 10.6 %collective-permute-done = bf16[16,64,128]{2,1,0:T(8,128)(2,1)S(1)} collective-permute-done((bf16[16,64,128]{2,1,0:T(8,128)(2,1)}, bf16[16,64,128]{2,1,0:T(8,128)(2,1)S(1)}, u32[]{:S(2)}, u32[]{:S(2)}) %collective-permute-start) | collective-permute-done | bytes 262176 | tf_op jit(solution)/shard_map/while/body/eval_jaxpr/ppermute | solution.py:13
  194.5 9.8 %collective-permute-done = bf16[16,64,128]{2,1,0:T(8,128)(2,1)S(1)} collective-permute-done((bf16[16,64,128]{2,1,0:T(8,128)(2,1)}, bf16[16,64,128]{2,1,0:T(8,128)(2,1)S(1)}, u32[]{:S(2)}, u32[]{:S(2)}) %collective-permute-start) | collective-permute-done | bytes 262176 | tf_op jit(solution)/shard_map/while/body/eval_jaxpr/ppermute | solution.py:13
  209.1 8.9 %collective-permute-done = bf16[16,64,128]{2,1,0:T(8,128)(2,1)S(1)} collective-permute-done((bf16[16,64,128]{2,1,0:T(8,128)(2,1)}, bf16[16,64,128]{2,1,0:T(8,128)(2,1)S(1)}, u32[]{:S(2)}, u32[]{:S(2)}) %collective-permute-start) | collective-permute-done | bytes 262176 | tf_op jit(solution)/shard_map/while/body/eval_jaxpr/ppermute | solution.py:13
  222.8 8.7 collective-permute-done
  236.3 8.7 collective-permute-done
  249.8 8.7 collective-permute-done
  263.3 8.7 collective-permute-done
  276.8 8.7 collective-permute-done
  290.3 8.7 collective-permute-done
  303.8 9.4 %collective-permute-done = bf16[16,64,128]{2,1,0:T(8,128)(2,1)S(1)} collective-permute-done((bf16[16,64,128]{2,1,0:T(8,128)(2,1)}, bf16[16,64,128]{2,1,0:T(8,128)(2,1)S(1)}, u32[]{:S(2)}, u32[]{:S(2)}) %collective-permute-start) | collective-permute-done | bytes 262176 | tf_op jit(solution)/shard_map/while/body/eval_jaxpr/ppermute | solution.py:13
  318.0 10.6 %collective-permute-done = bf16[16,64,128]{2,1,0:T(8,128)(2,1)S(1)} collective-permute-done((bf16[16,64,128]{2,1,0:T(8,128)(2,1)}, bf16[16,64,128]{2,1,0:T(8,128)(2,1)S(1)}, u32[]{:S(2)}, u32[]{:S(2)}) %collective-permute-start) | collective-permute-done | bytes 262176 | tf_op jit(solution)/shard_map/while/body/eval_jaxpr/ppermute | solution.py:13
  333.4 11.2 %collective-permute-done = bf16[16,64,128]{2,1,0:T(8,128)(2,1)S(1)} collective-permute-done((bf16[16,64,128]{2,1,0:T(8,128)(2,1)}, bf16[16,64,128]{2,1,0:T(8,128)(2,1)S(1)}, u32[]{:S(2)}, u32[]{:S(2)}) %collective-permute-start) | collective-permute-done | bytes 262176 | tf_op jit(solution)/shard_map/while/body/eval_jaxpr/ppermute | solution.py:13
  349.5 10.3 %collective-permute-done = bf16[16,64,128]{2,1,0:T(8,128)(2,1)S(1)} collective-permute-done((bf16[16,64,128]{2,1,0:T(8,128)(2,1)}, bf16[16,64,128]{2,1,0:T(8,128)(2,1)S(1)}, u32[]{:S(2)}, u32[]{:S(2)}) %collective-permute-start) | collective-permute-done | bytes 262176 | tf_op jit(solution)/shard_map/while/body/eval_jaxpr/ppermute | solution.py:13
  364.7 9.5 %collective-permute-done = bf16[16,64,128]{2,1,0:T(8,128)(2,1)S(1)} collective-permute-done((bf16[16,64,128]{2,1,0:T(8,128)(2,1)}, bf16[16,64,128]{2,1,0:T(8,128)(2,1)S(1)}, u32[]{:S(2)}, u32[]{:S(2)}) %collective-permute-start) | collective-permute-done | bytes 262176 | tf_op jit(solution)/shard_map/while/body/eval_jaxpr/ppermute | solution.py:13
  379.0 8.7 collective-permute-done
  420.1 8.0 collective-permute-start
  485.4 9.7 %all_to_all.20 = bf16[4,8,4096]{2,1,0:T(8,128)(2,1)} all-to-all(bf16[4,8,4096]{2,1,0:T(8,128)(2,1)S(1)} %convolution_convert_fusion.1), channel_id=1, replica_groups=mesh['seq'=32,'exp'=4,'dp'=2] {'exp'}, dimensions={0} | all-to-all | bytes 524288 | tf_op jit(solution)/shard_map/all_to_all | solution.py:84
  495.2 126.1 %all-gather.2.cloned.1.call-done = bf16[1024,4096]{1,0:T(8,128)(2,1)} async-done(((bf16[32,4096]{1,0:T(8,128)(2,1)}), bf16[1024,4096]{1,0:T(8,128)(2,1)}) %all-gather.2.cloned.1.call-update) | async-done | bytes 8388624 | tf_op jit(solution)/shard_map/all_gather | solution.py:89
  621.3 8.0 fusion.8
  642.9 226.2 %reduce-scatter.2.cloned.1.call-done = bf16[32,4096]{1,0:T(8,128)(2,1)} async-done(((bf16[1024,4096]{1,0:T(8,128)(2,1)}), bf16[32,4096]{1,0:T(8,128)(2,1)}) %reduce-scatter.2.cloned.1.call-update) | async-done | bytes 262160 | tf_op jit(solution)/shard_map/reduce_scatter | solution.py:94
  (164 shorter events, 256.0 us)
Async XLA Ops:
  22.2 12.2 %collective-permute-start = (bf16[16,64,128]{2,1,0:T(8,128)(2,1)}, bf16[16,64,128]{2,1,0:T(8,128)(2,1)S(1)}, u32[]{:S(2)}, u32[]{:S(2)}) collective-permute-start(bf16[16,64,128]{2,1,0:T(8,128)(2,1)} %fusion.54), channel_id=1, source_target_pairs={{0,8},{8,16},{16,24},{24,32},{32,40},{40,48},{48,56},{56,64},{64,7... | collective-permute-start | bytes 786440 | tf_op jit(solution)/shard_map/while/body/eval_jaxpr/ppermute | solution.py:13
  37.4 11.4 %collective-permute-start = (bf16[16,64,128]{2,1,0:T(8,128)(2,1)}, bf16[16,64,128]{2,1,0:T(8,128)(2,1)S(1)}, u32[]{:S(2)}, u32[]{:S(2)}) collective-permute-start(bf16[16,64,128]{2,1,0:T(8,128)(2,1)} %fusion.54), channel_id=1, source_target_pairs={{0,8},{8,16},{16,24},{24,32},{32,40},{40,48},{48,56},{56,64},{64,7... | collective-permute-start | bytes 786440 | tf_op jit(solution)/shard_map/while/body/eval_jaxpr/ppermute | solution.py:13
  51.7 10.6 %collective-permute-start = (bf16[16,64,128]{2,1,0:T(8,128)(2,1)}, bf16[16,64,128]{2,1,0:T(8,128)(2,1)S(1)}, u32[]{:S(2)}, u32[]{:S(2)}) collective-permute-start(bf16[16,64,128]{2,1,0:T(8,128)(2,1)} %fusion.54), channel_id=1, source_target_pairs={{0,8},{8,16},{16,24},{24,32},{32,40},{40,48},{48,56},{56,64},{64,7... | collective-permute-start | bytes 786440 | tf_op jit(solution)/shard_map/while/body/eval_jaxpr/ppermute | solution.py:13
  65.2 10.6 %collective-permute-start = (bf16[16,64,128]{2,1,0:T(8,128)(2,1)}, bf16[16,64,128]{2,1,0:T(8,128)(2,1)S(1)}, u32[]{:S(2)}, u32[]{:S(2)}) collective-permute-start(bf16[16,64,128]{2,1,0:T(8,128)(2,1)} %fusion.54), channel_id=1, source_target_pairs={{0,8},{8,16},{16,24},{24,32},{32,40},{40,48},{48,56},{56,64},{64,7... | collective-permute-start | bytes 786440 | tf_op jit(solution)/shard_map/while/body/eval_jaxpr/ppermute | solution.py:13
  78.6 10.6 %collective-permute-start = (bf16[16,64,128]{2,1,0:T(8,128)(2,1)}, bf16[16,64,128]{2,1,0:T(8,128)(2,1)S(1)}, u32[]{:S(2)}, u32[]{:S(2)}) collective-permute-start(bf16[16,64,128]{2,1,0:T(8,128)(2,1)} %fusion.54), channel_id=1, source_target_pairs={{0,8},{8,16},{16,24},{24,32},{32,40},{40,48},{48,56},{56,64},{64,7... | collective-permute-start | bytes 786440 | tf_op jit(solution)/shard_map/while/body/eval_jaxpr/ppermute | solution.py:13
  92.1 10.6 %collective-permute-start = (bf16[16,64,128]{2,1,0:T(8,128)(2,1)}, bf16[16,64,128]{2,1,0:T(8,128)(2,1)S(1)}, u32[]{:S(2)}, u32[]{:S(2)}) collective-permute-start(bf16[16,64,128]{2,1,0:T(8,128)(2,1)} %fusion.54), channel_id=1, source_target_pairs={{0,8},{8,16},{16,24},{24,32},{32,40},{40,48},{48,56},{56,64},{64,7... | collective-permute-start | bytes 786440 | tf_op jit(solution)/shard_map/while/body/eval_jaxpr/ppermute | solution.py:13
  105.6 10.6 %collective-permute-start = (bf16[16,64,128]{2,1,0:T(8,128)(2,1)}, bf16[16,64,128]{2,1,0:T(8,128)(2,1)S(1)}, u32[]{:S(2)}, u32[]{:S(2)}) collective-permute-start(bf16[16,64,128]{2,1,0:T(8,128)(2,1)} %fusion.54), channel_id=1, source_target_pairs={{0,8},{8,16},{16,24},{24,32},{32,40},{40,48},{48,56},{56,64},{64,7... | collective-permute-start | bytes 786440 | tf_op jit(solution)/shard_map/while/body/eval_jaxpr/ppermute | solution.py:13
  119.1 10.6 %collective-permute-start = (bf16[16,64,128]{2,1,0:T(8,128)(2,1)}, bf16[16,64,128]{2,1,0:T(8,128)(2,1)S(1)}, u32[]{:S(2)}, u32[]{:S(2)}) collective-permute-start(bf16[16,64,128]{2,1,0:T(8,128)(2,1)} %fusion.54), channel_id=1, source_target_pairs={{0,8},{8,16},{16,24},{24,32},{32,40},{40,48},{48,56},{56,64},{64,7... | collective-permute-start | bytes 786440 | tf_op jit(solution)/shard_map/while/body/eval_jaxpr/ppermute | solution.py:13
  132.6 10.8 %collective-permute-start = (bf16[16,64,128]{2,1,0:T(8,128)(2,1)}, bf16[16,64,128]{2,1,0:T(8,128)(2,1)S(1)}, u32[]{:S(2)}, u32[]{:S(2)}) collective-permute-start(bf16[16,64,128]{2,1,0:T(8,128)(2,1)} %fusion.54), channel_id=1, source_target_pairs={{0,8},{8,16},{16,24},{24,32},{32,40},{40,48},{48,56},{56,64},{64,7... | collective-permute-start | bytes 786440 | tf_op jit(solution)/shard_map/while/body/eval_jaxpr/ppermute | solution.py:13
  146.3 11.9 %collective-permute-start = (bf16[16,64,128]{2,1,0:T(8,128)(2,1)}, bf16[16,64,128]{2,1,0:T(8,128)(2,1)S(1)}, u32[]{:S(2)}, u32[]{:S(2)}) collective-permute-start(bf16[16,64,128]{2,1,0:T(8,128)(2,1)} %fusion.54), channel_id=1, source_target_pairs={{0,8},{8,16},{16,24},{24,32},{32,40},{40,48},{48,56},{56,64},{64,7... | collective-permute-start | bytes 786440 | tf_op jit(solution)/shard_map/while/body/eval_jaxpr/ppermute | solution.py:13
  161.1 13.1 %collective-permute-start = (bf16[16,64,128]{2,1,0:T(8,128)(2,1)}, bf16[16,64,128]{2,1,0:T(8,128)(2,1)S(1)}, u32[]{:S(2)}, u32[]{:S(2)}) collective-permute-start(bf16[16,64,128]{2,1,0:T(8,128)(2,1)} %fusion.54), channel_id=1, source_target_pairs={{0,8},{8,16},{16,24},{24,32},{32,40},{40,48},{48,56},{56,64},{64,7... | collective-permute-start | bytes 786440 | tf_op jit(solution)/shard_map/while/body/eval_jaxpr/ppermute | solution.py:13
  177.1 12.5 %collective-permute-start = (bf16[16,64,128]{2,1,0:T(8,128)(2,1)}, bf16[16,64,128]{2,1,0:T(8,128)(2,1)S(1)}, u32[]{:S(2)}, u32[]{:S(2)}) collective-permute-start(bf16[16,64,128]{2,1,0:T(8,128)(2,1)} %fusion.54), channel_id=1, source_target_pairs={{0,8},{8,16},{16,24},{24,32},{32,40},{40,48},{48,56},{56,64},{64,7... | collective-permute-start | bytes 786440 | tf_op jit(solution)/shard_map/while/body/eval_jaxpr/ppermute | solution.py:13
  192.6 11.7 %collective-permute-start = (bf16[16,64,128]{2,1,0:T(8,128)(2,1)}, bf16[16,64,128]{2,1,0:T(8,128)(2,1)S(1)}, u32[]{:S(2)}, u32[]{:S(2)}) collective-permute-start(bf16[16,64,128]{2,1,0:T(8,128)(2,1)} %fusion.54), channel_id=1, source_target_pairs={{0,8},{8,16},{16,24},{24,32},{32,40},{40,48},{48,56},{56,64},{64,7... | collective-permute-start | bytes 786440 | tf_op jit(solution)/shard_map/while/body/eval_jaxpr/ppermute | solution.py:13
  207.2 10.8 %collective-permute-start = (bf16[16,64,128]{2,1,0:T(8,128)(2,1)}, bf16[16,64,128]{2,1,0:T(8,128)(2,1)S(1)}, u32[]{:S(2)}, u32[]{:S(2)}) collective-permute-start(bf16[16,64,128]{2,1,0:T(8,128)(2,1)} %fusion.54), channel_id=1, source_target_pairs={{0,8},{8,16},{16,24},{24,32},{32,40},{40,48},{48,56},{56,64},{64,7... | collective-permute-start | bytes 786440 | tf_op jit(solution)/shard_map/while/body/eval_jaxpr/ppermute | solution.py:13
  247.9 10.6 %collective-permute-start = (bf16[16,64,128]{2,1,0:T(8,128)(2,1)}, bf16[16,64,128]{2,1,0:T(8,128)(2,1)S(1)}, u32[]{:S(2)}, u32[]{:S(2)}) collective-permute-start(bf16[16,64,128]{2,1,0:T(8,128)(2,1)} %fusion.54), channel_id=1, source_target_pairs={{0,8},{8,16},{16,24},{24,32},{32,40},{40,48},{48,56},{56,64},{64,7... | collective-permute-start | bytes 786440 | tf_op jit(solution)/shard_map/while/body/eval_jaxpr/ppermute | solution.py:13
  261.4 10.6 %collective-permute-start = (bf16[16,64,128]{2,1,0:T(8,128)(2,1)}, bf16[16,64,128]{2,1,0:T(8,128)(2,1)S(1)}, u32[]{:S(2)}, u32[]{:S(2)}) collective-permute-start(bf16[16,64,128]{2,1,0:T(8,128)(2,1)} %fusion.54), channel_id=1, source_target_pairs={{0,8},{8,16},{16,24},{24,32},{32,40},{40,48},{48,56},{56,64},{64,7... | collective-permute-start | bytes 786440 | tf_op jit(solution)/shard_map/while/body/eval_jaxpr/ppermute | solution.py:13
  274.9 10.6 %collective-permute-start = (bf16[16,64,128]{2,1,0:T(8,128)(2,1)}, bf16[16,64,128]{2,1,0:T(8,128)(2,1)S(1)}, u32[]{:S(2)}, u32[]{:S(2)}) collective-permute-start(bf16[16,64,128]{2,1,0:T(8,128)(2,1)} %fusion.54), channel_id=1, source_target_pairs={{0,8},{8,16},{16,24},{24,32},{32,40},{40,48},{48,56},{56,64},{64,7... | collective-permute-start | bytes 786440 | tf_op jit(solution)/shard_map/while/body/eval_jaxpr/ppermute | solution.py:13
  288.4 10.6 %collective-permute-start = (bf16[16,64,128]{2,1,0:T(8,128)(2,1)}, bf16[16,64,128]{2,1,0:T(8,128)(2,1)S(1)}, u32[]{:S(2)}, u32[]{:S(2)}) collective-permute-start(bf16[16,64,128]{2,1,0:T(8,128)(2,1)} %fusion.54), channel_id=1, source_target_pairs={{0,8},{8,16},{16,24},{24,32},{32,40},{40,48},{48,56},{56,64},{64,7... | collective-permute-start | bytes 786440 | tf_op jit(solution)/shard_map/while/body/eval_jaxpr/ppermute | solution.py:13
  301.9 11.3 %collective-permute-start = (bf16[16,64,128]{2,1,0:T(8,128)(2,1)}, bf16[16,64,128]{2,1,0:T(8,128)(2,1)S(1)}, u32[]{:S(2)}, u32[]{:S(2)}) collective-permute-start(bf16[16,64,128]{2,1,0:T(8,128)(2,1)} %fusion.54), channel_id=1, source_target_pairs={{0,8},{8,16},{16,24},{24,32},{32,40},{40,48},{48,56},{56,64},{64,7... | collective-permute-start | bytes 786440 | tf_op jit(solution)/shard_map/while/body/eval_jaxpr/ppermute | solution.py:13
  316.1 12.5 %collective-permute-start = (bf16[16,64,128]{2,1,0:T(8,128)(2,1)}, bf16[16,64,128]{2,1,0:T(8,128)(2,1)S(1)}, u32[]{:S(2)}, u32[]{:S(2)}) collective-permute-start(bf16[16,64,128]{2,1,0:T(8,128)(2,1)} %fusion.54), channel_id=1, source_target_pairs={{0,8},{8,16},{16,24},{24,32},{32,40},{40,48},{48,56},{56,64},{64,7... | collective-permute-start | bytes 786440 | tf_op jit(solution)/shard_map/while/body/eval_jaxpr/ppermute | solution.py:13
  331.5 13.1 %collective-permute-start = (bf16[16,64,128]{2,1,0:T(8,128)(2,1)}, bf16[16,64,128]{2,1,0:T(8,128)(2,1)S(1)}, u32[]{:S(2)}, u32[]{:S(2)}) collective-permute-start(bf16[16,64,128]{2,1,0:T(8,128)(2,1)} %fusion.54), channel_id=1, source_target_pairs={{0,8},{8,16},{16,24},{24,32},{32,40},{40,48},{48,56},{56,64},{64,7... | collective-permute-start | bytes 786440 | tf_op jit(solution)/shard_map/while/body/eval_jaxpr/ppermute | solution.py:13
  347.6 12.3 %collective-permute-start = (bf16[16,64,128]{2,1,0:T(8,128)(2,1)}, bf16[16,64,128]{2,1,0:T(8,128)(2,1)S(1)}, u32[]{:S(2)}, u32[]{:S(2)}) collective-permute-start(bf16[16,64,128]{2,1,0:T(8,128)(2,1)} %fusion.54), channel_id=1, source_target_pairs={{0,8},{8,16},{16,24},{24,32},{32,40},{40,48},{48,56},{56,64},{64,7... | collective-permute-start | bytes 786440 | tf_op jit(solution)/shard_map/while/body/eval_jaxpr/ppermute | solution.py:13
  362.7 11.4 %collective-permute-start = (bf16[16,64,128]{2,1,0:T(8,128)(2,1)}, bf16[16,64,128]{2,1,0:T(8,128)(2,1)S(1)}, u32[]{:S(2)}, u32[]{:S(2)}) collective-permute-start(bf16[16,64,128]{2,1,0:T(8,128)(2,1)} %fusion.54), channel_id=1, source_target_pairs={{0,8},{8,16},{16,24},{24,32},{32,40},{40,48},{48,56},{56,64},{64,7... | collective-permute-start | bytes 786440 | tf_op jit(solution)/shard_map/while/body/eval_jaxpr/ppermute | solution.py:13
  377.1 10.6 %collective-permute-start = (bf16[16,64,128]{2,1,0:T(8,128)(2,1)}, bf16[16,64,128]{2,1,0:T(8,128)(2,1)S(1)}, u32[]{:S(2)}, u32[]{:S(2)}) collective-permute-start(bf16[16,64,128]{2,1,0:T(8,128)(2,1)} %fusion.54), channel_id=1, source_target_pairs={{0,8},{8,16},{16,24},{24,32},{32,40},{40,48},{48,56},{56,64},{64,7... | collective-permute-start | bytes 786440 | tf_op jit(solution)/shard_map/while/body/eval_jaxpr/ppermute | solution.py:13
  404.0 13.2 %collective-permute-start = (bf16[16,64,128]{2,1,0:T(8,128)(2,1)}, bf16[16,64,128]{2,1,0:T(8,128)(2,1)S(1)}, u32[]{:S(2)}, u32[]{:S(2)}) collective-permute-start(bf16[16,64,128]{2,1,0:T(8,128)(2,1)} %fusion.54), channel_id=1, source_target_pairs={{0,8},{8,16},{16,24},{24,32},{32,40},{40,48},{48,56},{56,64},{64,7... | collective-permute-start | bytes 786440 | tf_op jit(solution)/shard_map/while/body/eval_jaxpr/ppermute | solution.py:13
  420.1 12.3 %collective-permute-start = (bf16[16,64,128]{2,1,0:T(8,128)(2,1)}, bf16[16,64,128]{2,1,0:T(8,128)(2,1)S(1)}, u32[]{:S(2)}, u32[]{:S(2)}) collective-permute-start(bf16[16,64,128]{2,1,0:T(8,128)(2,1)} %fusion.54), channel_id=1, source_target_pairs={{0,8},{8,16},{16,24},{24,32},{32,40},{40,48},{48,56},{56,64},{64,7... | collective-permute-start | bytes 786440 | tf_op jit(solution)/shard_map/while/body/eval_jaxpr/ppermute | solution.py:13
  435.3 11.6 %collective-permute-start = (bf16[16,64,128]{2,1,0:T(8,128)(2,1)}, bf16[16,64,128]{2,1,0:T(8,128)(2,1)S(1)}, u32[]{:S(2)}, u32[]{:S(2)}) collective-permute-start(bf16[16,64,128]{2,1,0:T(8,128)(2,1)} %fusion.54), channel_id=1, source_target_pairs={{0,8},{8,16},{16,24},{24,32},{32,40},{40,48},{48,56},{56,64},{64,7... | collective-permute-start | bytes 786440 | tf_op jit(solution)/shard_map/while/body/eval_jaxpr/ppermute | solution.py:13
  449.9 11.5 %collective-permute-start = (bf16[16,64,128]{2,1,0:T(8,128)(2,1)}, bf16[16,64,128]{2,1,0:T(8,128)(2,1)S(1)}, u32[]{:S(2)}, u32[]{:S(2)}) collective-permute-start(bf16[16,64,128]{2,1,0:T(8,128)(2,1)} %fusion.54), channel_id=1, source_target_pairs={{0,8},{8,16},{16,24},{24,32},{32,40},{40,48},{48,56},{56,64},{64,7... | collective-permute-start | bytes 786440 | tf_op jit(solution)/shard_map/while/body/eval_jaxpr/ppermute | solution.py:13
  470.2 12.5 %all-to-all-start = ((bf16[4,64,1024]{2,1,0:T(8,128)(2,1)}), bf16[4,64,1024]{2,1,0:T(8,128)(2,1)}, u32[]{:S(2)}, u32[]{:S(2)}) async-start(bf16[4,64,1024]{2,1,0:T(8,128)(2,1)} %copy.30), calls=%async_computation | async-start | bytes 1048576 | tf_op jit(solution)/shard_map/all_to_all | solution.py:57
  474.5 146.8 %all-gather.2.cloned.1.call-start = ((), (), s32[]{:S(2)}) async-start(), calls=%async_computation.4 | async-start | bytes 8650752 | tf_op jit(solution)/shard_map/all_gather | solution.py:89
  495.1 373.9 %reduce-scatter.2.cloned.1.call-start = ((), (), s32[]{:S(2)}) async-start(), calls=%async_computation.5 | async-start | bytes 8650752 | tf_op jit(solution)/shard_map/reduce_scatter | solution.py:94
  869.1 11.0 %all-to-all-start.2 = ((bf16[4,8,4096]{2,1,0:T(8,128)(2,1)}), bf16[4,8,4096]{2,1,0:T(8,128)(2,1)S(1)}, u32[]{:S(2)}, u32[]{:S(2)}) async-start(bf16[4,8,4096]{2,1,0:T(8,128)(2,1)} %bitcast.84), calls=%async_computation.3 | async-start | bytes 524288 | tf_op jit(solution)/shard_map/all_to_all | solution.py:101
  (15 other events, 1589.6 us)
Sparse Core Ops, SparseCore 0:
  495.3 126.0 all-gather.1
  640.7 228.3 reduce-scatter.1
where the time goes:
time: 891 us; the launch traced here: 889 us
  waiting for transfers between devices  633 us (71%)
  other arithmetic  94.9 us (11%)
  starting transfers between devices  93.5 us (10%)
  matrix products  33.1 us (4%)
  between operations  13.6 us (2%)
  local copies, waits for them, and re-layouts  10.6 us (1%)
  blocking collectives  9.75 us (1%)
    ppermute x31, waiting for transfers between devices, shifted(): return lax.ppermute(block, axis, route)  267 us
    reduce_scatter x1, waiting for transfers between devices, body(): lax.psum_scatter(jnp.dot(fragment, down_part, preferred_element_type=jnp....  226 us
    all_gather x1, waiting for transfers between devices, body(): fragment = lax.all_gather(routed, 'seq', axis=0, tiled=True)  126 us
    ppermute x31, starting transfers between devices, shifted(): return lax.ppermute(block, axis, route)  84.9 us
    convert_element_type x31, other arithmetic, advance(): outgoing.astype(jnp.bfloat16)  63.5 us
    convert_element_type x31, other arithmetic, advance(): shifted(outgoing.astype(jnp.bfloat16), 'seq', 1).astype(outgoing.dtype)  26.7 us
  transfers between devices with their start and end apart: 35, of which 35 were waited for; matrix products, arithmetic and copies ran while one was open for 0% of the time, Pallas kernels for 0%

commit v1 on v0

--- a/solution.py
+++ b/solution.py
@@ -86,7 +86,9 @@
     gate_part = gate_weight[0]
     up_part = up_weight[0]
     down_part = down_weight[0]
-    fragment = lax.all_gather(routed, "seq", axis=0, tiled=True)
+    fragment = jnp.concatenate(
+        lax.all_to_all(jnp.stack([routed] * lax.axis_size("seq")), "seq", 0, 0), axis=0
+    )
     gated = jnp.dot(fragment, gate_part, preferred_element_type=jnp.float32)
     lifted = jnp.dot(fragment, up_part, preferred_element_type=jnp.float32)
     hidden_all = (jax.nn.silu(gated) * lifted).astype(jnp.bfloat16)

time: 891 us -> 948 us (1.064)
  blocking collectives: 9.75 us -> 198 us
  waiting for transfers between devices: 633 us -> 505 us
    all_to_all x0 -> x1, blocking collectives: none -> 189 us  [body(): lax.all_to_all(jnp.stack([routed] * lax.axis_size('seq')), 'seq', 0, 0)]
    all_gather x1 -> x0, waiting for transfers between devices: 126 us -> none  [body(): fragment = lax.all_gather(routed, 'seq', axis=0, tiled=True)]
  transfers between devices with their start and end apart: 35 -> 34, of which waited for: 35 -> 34; matrix products, arithmetic and copies ran while one was open for 0% -> 0% of each run, Pallas kernels for 0% -> 0%
where the time goes in v1:
time: 948 us; the launch traced here: 946 us
  waiting for transfers between devices  505 us (53%)
  blocking collectives  198 us (21%)
  other arithmetic  94.9 us (10%)
  starting transfers between devices  93.5 us (10%)
  matrix products  29.6 us (3%)
  between operations  13.6 us (1%)
  local copies, waits for them, and re-layouts  10.9 us (1%)
    ppermute x31, waiting for transfers between devices, shifted(): return lax.ppermute(block, axis, route)  267 us
    reduce_scatter x1, waiting for transfers between devices, body(): lax.psum_scatter(jnp.dot(fragment, down_part, preferred_element_type=jnp....  224 us
    all_to_all x1, blocking collectives, body(): lax.all_to_all(jnp.stack([routed] * lax.axis_size('seq')), 'seq', 0, 0)  189 us
    ppermute x31, starting transfers between devices, shifted(): return lax.ppermute(block, axis, route)  84.9 us
    convert_element_type x31, other arithmetic, advance(): outgoing.astype(jnp.bfloat16)  63.5 us
    convert_element_type x31, other arithmetic, advance(): shifted(outgoing.astype(jnp.bfloat16), 'seq', 1).astype(outgoing.dtype)  26.7 us
  transfers between devices with their start and end apart: 34, of which 34 were waited for; matrix products, arithmetic and copies ran while one was open for 0% of the time, Pallas kernels for 0%

profile of v1, /device:TPU:64, one launch (start us, length us, event | category | flops | bytes accessed | tf_op | source)
XLA Modules:
  0.0 945.7 jit_solution(8559393438891140684)
XLA Ops:
  20.3 442.0 %while.11 = (s32[]{:T(128)}, f32[16,64,128]{2,1,0:T(8,128)}, f32[16]{0:T(128)S(1)}, f32[16,64,128]{2,1,0:T(8,128)}, s32[]{:T(128)}, /*index=5*/s32[]{:T(128)}) while((s32[]{:T(128)}, f32[16,64,128]{2,1,0:T(8,128)}, f32[16]{0:T(128)S(1)}, f32[16,64,128]{2,1,0:T(8,128)}, s32[]{:T(128)}, /*index=5*/s32[]{:T(128)}) %tuple.31), condition=%wide.region_3.4_spmd.clone, body=%wide.region_2.3_spmd.clone.sunk | while | flops 655363 | bytes 3145911 | solution.py:50
  25.7 8.8 collective-permute-done
  39.3 9.5 %collective-permute-done = bf16[16,64,128]{2,1,0:T(8,128)(2,1)S(1)} collective-permute-done((bf16[16,64,128]{2,1,0:T(8,128)(2,1)}, bf16[16,64,128]{2,1,0:T(8,128)(2,1)S(1)}, u32[]{:S(2)}, u32[]{:S(2)}) %collective-permute-start) | collective-permute-done | bytes 262176 | tf_op jit(solution)/shard_map/while/body/eval_jaxpr/ppermute | solution.py:13
  53.6 8.7 collective-permute-done
  67.1 8.7 collective-permute-done
  80.6 8.7 collective-permute-done
  94.1 8.7 collective-permute-done
  107.5 8.7 collective-permute-done
  121.0 8.7 collective-permute-done
  134.5 8.9 collective-permute-done
  148.2 10.0 %collective-permute-done = bf16[16,64,128]{2,1,0:T(8,128)(2,1)S(1)} collective-permute-done((bf16[16,64,128]{2,1,0:T(8,128)(2,1)}, bf16[16,64,128]{2,1,0:T(8,128)(2,1)S(1)}, u32[]{:S(2)}, u32[]{:S(2)}) %collective-permute-start) | collective-permute-done | bytes 262176 | tf_op jit(solution)/shard_map/while/body/eval_jaxpr/ppermute | solution.py:13
  163.1 11.2 %collective-permute-done = bf16[16,64,128]{2,1,0:T(8,128)(2,1)S(1)} collective-permute-done((bf16[16,64,128]{2,1,0:T(8,128)(2,1)}, bf16[16,64,128]{2,1,0:T(8,128)(2,1)S(1)}, u32[]{:S(2)}, u32[]{:S(2)}) %collective-permute-start) | collective-permute-done | bytes 262176 | tf_op jit(solution)/shard_map/while/body/eval_jaxpr/ppermute | solution.py:13
  179.0 10.6 %collective-permute-done = bf16[16,64,128]{2,1,0:T(8,128)(2,1)S(1)} collective-permute-done((bf16[16,64,128]{2,1,0:T(8,128)(2,1)}, bf16[16,64,128]{2,1,0:T(8,128)(2,1)S(1)}, u32[]{:S(2)}, u32[]{:S(2)}) %collective-permute-start) | collective-permute-done | bytes 262176 | tf_op jit(solution)/shard_map/while/body/eval_jaxpr/ppermute | solution.py:13
  194.5 9.8 %collective-permute-done = bf16[16,64,128]{2,1,0:T(8,128)(2,1)S(1)} collective-permute-done((bf16[16,64,128]{2,1,0:T(8,128)(2,1)}, bf16[16,64,128]{2,1,0:T(8,128)(2,1)S(1)}, u32[]{:S(2)}, u32[]{:S(2)}) %collective-permute-start) | collective-permute-done | bytes 262176 | tf_op jit(solution)/shard_map/while/body/eval_jaxpr/ppermute | solution.py:13
  209.1 8.9 collective-permute-done
  222.8 8.7 collective-permute-done
  236.3 8.7 collective-permute-done
  249.8 8.7 collective-permute-done
  263.3 8.7 collective-permute-done
  276.8 8.7 collective-permute-done
  290.3 8.7 collective-permute-done
  303.8 9.4 collective-permute-done
  318.0 10.6 %collective-permute-done = bf16[16,64,128]{2,1,0:T(8,128)(2,1)S(1)} collective-permute-done((bf16[16,64,128]{2,1,0:T(8,128)(2,1)}, bf16[16,64,128]{2,1,0:T(8,128)(2,1)S(1)}, u32[]{:S(2)}, u32[]{:S(2)}) %collective-permute-start) | collective-permute-done | bytes 262176 | tf_op jit(solution)/shard_map/while/body/eval_jaxpr/ppermute | solution.py:13
  333.4 11.2 %collective-permute-done = bf16[16,64,128]{2,1,0:T(8,128)(2,1)S(1)} collective-permute-done((bf16[16,64,128]{2,1,0:T(8,128)(2,1)}, bf16[16,64,128]{2,1,0:T(8,128)(2,1)S(1)}, u32[]{:S(2)}, u32[]{:S(2)}) %collective-permute-start) | collective-permute-done | bytes 262176 | tf_op jit(solution)/shard_map/while/body/eval_jaxpr/ppermute | solution.py:13
  349.5 10.3 %collective-permute-done = bf16[16,64,128]{2,1,0:T(8,128)(2,1)S(1)} collective-permute-done((bf16[16,64,128]{2,1,0:T(8,128)(2,1)}, bf16[16,64,128]{2,1,0:T(8,128)(2,1)S(1)}, u32[]{:S(2)}, u32[]{:S(2)}) %collective-permute-start) | collective-permute-done | bytes 262176 | tf_op jit(solution)/shard_map/while/body/eval_jaxpr/ppermute | solution.py:13
  364.7 9.5 %collective-permute-done = bf16[16,64,128]{2,1,0:T(8,128)(2,1)S(1)} collective-permute-done((bf16[16,64,128]{2,1,0:T(8,128)(2,1)}, bf16[16,64,128]{2,1,0:T(8,128)(2,1)S(1)}, u32[]{:S(2)}, u32[]{:S(2)}) %collective-permute-start) | collective-permute-done | bytes 262176 | tf_op jit(solution)/shard_map/while/body/eval_jaxpr/ppermute | solution.py:13
  379.0 8.7 collective-permute-done
  420.1 8.0 collective-permute-start
  474.9 7.8 all-to-all-done
  484.6 9.1 all_to_all.25
  494.7 188.9 %all_to_all.26 = bf16[32,32,4096]{2,1,0:T(8,128)(2,1)S(1)} all-to-all(bf16[32,32,4096]{2,1,0:T(8,128)(2,1)S(1)} %stack.3), channel_id=1, replica_groups=mesh['seq'=32,'exp'=4,'dp'=2] {'seq'}, dimensions={0} | all-to-all | bytes 16777216 | tf_op jit(solution)/shard_map/all_to_all | solution.py:90
  701.7 224.0 %reduce-scatter.2.cloned.1.call-done = bf16[32,4096]{1,0:T(8,128)(2,1)} async-done(((bf16[1024,4096]{1,0:T(8,128)(2,1)}), bf16[32,4096]{1,0:T(8,128)(2,1)}) %reduce-scatter.2.cloned.1.call-update) | async-done | bytes 262160 | tf_op jit(solution)/shard_map/reduce_scatter | solution.py:96
  (163 shorter events, 252.9 us)
Async XLA Ops:
  22.2 12.2 %collective-permute-start = (bf16[16,64,128]{2,1,0:T(8,128)(2,1)}, bf16[16,64,128]{2,1,0:T(8,128)(2,1)S(1)}, u32[]{:S(2)}, u32[]{:S(2)}) collective-permute-start(bf16[16,64,128]{2,1,0:T(8,128)(2,1)} %fusion.54), channel_id=1, source_target_pairs={{0,8},{8,16},{16,24},{24,32},{32,40},{40,48},{48,56},{56,64},{64,7... | collective-permute-start | bytes 786440 | tf_op jit(solution)/shard_map/while/body/eval_jaxpr/ppermute | solution.py:13
  37.4 11.4 %collective-permute-start = (bf16[16,64,128]{2,1,0:T(8,128)(2,1)}, bf16[16,64,128]{2,1,0:T(8,128)(2,1)S(1)}, u32[]{:S(2)}, u32[]{:S(2)}) collective-permute-start(bf16[16,64,128]{2,1,0:T(8,128)(2,1)} %fusion.54), channel_id=1, source_target_pairs={{0,8},{8,16},{16,24},{24,32},{32,40},{40,48},{48,56},{56,64},{64,7... | collective-permute-start | bytes 786440 | tf_op jit(solution)/shard_map/while/body/eval_jaxpr/ppermute | solution.py:13
  51.7 10.6 %collective-permute-start = (bf16[16,64,128]{2,1,0:T(8,128)(2,1)}, bf16[16,64,128]{2,1,0:T(8,128)(2,1)S(1)}, u32[]{:S(2)}, u32[]{:S(2)}) collective-permute-start(bf16[16,64,128]{2,1,0:T(8,128)(2,1)} %fusion.54), channel_id=1, source_target_pairs={{0,8},{8,16},{16,24},{24,32},{32,40},{40,48},{48,56},{56,64},{64,7... | collective-permute-start | bytes 786440 | tf_op jit(solution)/shard_map/while/body/eval_jaxpr/ppermute | solution.py:13
  65.2 10.6 %collective-permute-start = (bf16[16,64,128]{2,1,0:T(8,128)(2,1)}, bf16[16,64,128]{2,1,0:T(8,128)(2,1)S(1)}, u32[]{:S(2)}, u32[]{:S(2)}) collective-permute-start(bf16[16,64,128]{2,1,0:T(8,128)(2,1)} %fusion.54), channel_id=1, source_target_pairs={{0,8},{8,16},{16,24},{24,32},{32,40},{40,48},{48,56},{56,64},{64,7... | collective-permute-start | bytes 786440 | tf_op jit(solution)/shard_map/while/body/eval_jaxpr/ppermute | solution.py:13
  78.6 10.6 %collective-permute-start = (bf16[16,64,128]{2,1,0:T(8,128)(2,1)}, bf16[16,64,128]{2,1,0:T(8,128)(2,1)S(1)}, u32[]{:S(2)}, u32[]{:S(2)}) collective-permute-start(bf16[16,64,128]{2,1,0:T(8,128)(2,1)} %fusion.54), channel_id=1, source_target_pairs={{0,8},{8,16},{16,24},{24,32},{32,40},{40,48},{48,56},{56,64},{64,7... | collective-permute-start | bytes 786440 | tf_op jit(solution)/shard_map/while/body/eval_jaxpr/ppermute | solution.py:13
  92.1 10.6 %collective-permute-start = (bf16[16,64,128]{2,1,0:T(8,128)(2,1)}, bf16[16,64,128]{2,1,0:T(8,128)(2,1)S(1)}, u32[]{:S(2)}, u32[]{:S(2)}) collective-permute-start(bf16[16,64,128]{2,1,0:T(8,128)(2,1)} %fusion.54), channel_id=1, source_target_pairs={{0,8},{8,16},{16,24},{24,32},{32,40},{40,48},{48,56},{56,64},{64,7... | collective-permute-start | bytes 786440 | tf_op jit(solution)/shard_map/while/body/eval_jaxpr/ppermute | solution.py:13
  105.6 10.6 %collective-permute-start = (bf16[16,64,128]{2,1,0:T(8,128)(2,1)}, bf16[16,64,128]{2,1,0:T(8,128)(2,1)S(1)}, u32[]{:S(2)}, u32[]{:S(2)}) collective-permute-start(bf16[16,64,128]{2,1,0:T(8,128)(2,1)} %fusion.54), channel_id=1, source_target_pairs={{0,8},{8,16},{16,24},{24,32},{32,40},{40,48},{48,56},{56,64},{64,7... | collective-permute-start | bytes 786440 | tf_op jit(solution)/shard_map/while/body/eval_jaxpr/ppermute | solution.py:13
  119.1 10.6 %collective-permute-start = (bf16[16,64,128]{2,1,0:T(8,128)(2,1)}, bf16[16,64,128]{2,1,0:T(8,128)(2,1)S(1)}, u32[]{:S(2)}, u32[]{:S(2)}) collective-permute-start(bf16[16,64,128]{2,1,0:T(8,128)(2,1)} %fusion.54), channel_id=1, source_target_pairs={{0,8},{8,16},{16,24},{24,32},{32,40},{40,48},{48,56},{56,64},{64,7... | collective-permute-start | bytes 786440 | tf_op jit(solution)/shard_map/while/body/eval_jaxpr/ppermute | solution.py:13
  132.6 10.8 %collective-permute-start = (bf16[16,64,128]{2,1,0:T(8,128)(2,1)}, bf16[16,64,128]{2,1,0:T(8,128)(2,1)S(1)}, u32[]{:S(2)}, u32[]{:S(2)}) collective-permute-start(bf16[16,64,128]{2,1,0:T(8,128)(2,1)} %fusion.54), channel_id=1, source_target_pairs={{0,8},{8,16},{16,24},{24,32},{32,40},{40,48},{48,56},{56,64},{64,7... | collective-permute-start | bytes 786440 | tf_op jit(solution)/shard_map/while/body/eval_jaxpr/ppermute | solution.py:13
  146.3 11.9 %collective-permute-start = (bf16[16,64,128]{2,1,0:T(8,128)(2,1)}, bf16[16,64,128]{2,1,0:T(8,128)(2,1)S(1)}, u32[]{:S(2)}, u32[]{:S(2)}) collective-permute-start(bf16[16,64,128]{2,1,0:T(8,128)(2,1)} %fusion.54), channel_id=1, source_target_pairs={{0,8},{8,16},{16,24},{24,32},{32,40},{40,48},{48,56},{56,64},{64,7... | collective-permute-start | bytes 786440 | tf_op jit(solution)/shard_map/while/body/eval_jaxpr/ppermute | solution.py:13
  161.1 13.1 %collective-permute-start = (bf16[16,64,128]{2,1,0:T(8,128)(2,1)}, bf16[16,64,128]{2,1,0:T(8,128)(2,1)S(1)}, u32[]{:S(2)}, u32[]{:S(2)}) collective-permute-start(bf16[16,64,128]{2,1,0:T(8,128)(2,1)} %fusion.54), channel_id=1, source_target_pairs={{0,8},{8,16},{16,24},{24,32},{32,40},{40,48},{48,56},{56,64},{64,7... | collective-permute-start | bytes 786440 | tf_op jit(solution)/shard_map/while/body/eval_jaxpr/ppermute | solution.py:13
  177.1 12.5 %collective-permute-start = (bf16[16,64,128]{2,1,0:T(8,128)(2,1)}, bf16[16,64,128]{2,1,0:T(8,128)(2,1)S(1)}, u32[]{:S(2)}, u32[]{:S(2)}) collective-permute-start(bf16[16,64,128]{2,1,0:T(8,128)(2,1)} %fusion.54), channel_id=1, source_target_pairs={{0,8},{8,16},{16,24},{24,32},{32,40},{40,48},{48,56},{56,64},{64,7... | collective-permute-start | bytes 786440 | tf_op jit(solution)/shard_map/while/body/eval_jaxpr/ppermute | solution.py:13
  192.6 11.7 %collective-permute-start = (bf16[16,64,128]{2,1,0:T(8,128)(2,1)}, bf16[16,64,128]{2,1,0:T(8,128)(2,1)S(1)}, u32[]{:S(2)}, u32[]{:S(2)}) collective-permute-start(bf16[16,64,128]{2,1,0:T(8,128)(2,1)} %fusion.54), channel_id=1, source_target_pairs={{0,8},{8,16},{16,24},{24,32},{32,40},{40,48},{48,56},{56,64},{64,7... | collective-permute-start | bytes 786440 | tf_op jit(solution)/shard_map/while/body/eval_jaxpr/ppermute | solution.py:13
  207.2 10.8 %collective-permute-start = (bf16[16,64,128]{2,1,0:T(8,128)(2,1)}, bf16[16,64,128]{2,1,0:T(8,128)(2,1)S(1)}, u32[]{:S(2)}, u32[]{:S(2)}) collective-permute-start(bf16[16,64,128]{2,1,0:T(8,128)(2,1)} %fusion.54), channel_id=1, source_target_pairs={{0,8},{8,16},{16,24},{24,32},{32,40},{40,48},{48,56},{56,64},{64,7... | collective-permute-start | bytes 786440 | tf_op jit(solution)/shard_map/while/body/eval_jaxpr/ppermute | solution.py:13
  220.9 10.6 %collective-permute-start = (bf16[16,64,128]{2,1,0:T(8,128)(2,1)}, bf16[16,64,128]{2,1,0:T(8,128)(2,1)S(1)}, u32[]{:S(2)}, u32[]{:S(2)}) collective-permute-start(bf16[16,64,128]{2,1,0:T(8,128)(2,1)} %fusion.54), channel_id=1, source_target_pairs={{0,8},{8,16},{16,24},{24,32},{32,40},{40,48},{48,56},{56,64},{64,7... | collective-permute-start | bytes 786440 | tf_op jit(solution)/shard_map/while/body/eval_jaxpr/ppermute | solution.py:13
  234.4 10.6 %collective-permute-start = (bf16[16,64,128]{2,1,0:T(8,128)(2,1)}, bf16[16,64,128]{2,1,0:T(8,128)(2,1)S(1)}, u32[]{:S(2)}, u32[]{:S(2)}) collective-permute-start(bf16[16,64,128]{2,1,0:T(8,128)(2,1)} %fusion.54), channel_id=1, source_target_pairs={{0,8},{8,16},{16,24},{24,32},{32,40},{40,48},{48,56},{56,64},{64,7... | collective-permute-start | bytes 786440 | tf_op jit(solution)/shard_map/while/body/eval_jaxpr/ppermute | solution.py:13
  247.9 10.6 %collective-permute-start = (bf16[16,64,128]{2,1,0:T(8,128)(2,1)}, bf16[16,64,128]{2,1,0:T(8,128)(2,1)S(1)}, u32[]{:S(2)}, u32[]{:S(2)}) collective-permute-start(bf16[16,64,128]{2,1,0:T(8,128)(2,1)} %fusion.54), channel_id=1, source_target_pairs={{0,8},{8,16},{16,24},{24,32},{32,40},{40,48},{48,56},{56,64},{64,7... | collective-permute-start | bytes 786440 | tf_op jit(solution)/shard_map/while/body/eval_jaxpr/ppermute | solution.py:13
  261.4 10.6 %collective-permute-start = (bf16[16,64,128]{2,1,0:T(8,128)(2,1)}, bf16[16,64,128]{2,1,0:T(8,128)(2,1)S(1)}, u32[]{:S(2)}, u32[]{:S(2)}) collective-permute-start(bf16[16,64,128]{2,1,0:T(8,128)(2,1)} %fusion.54), channel_id=1, source_target_pairs={{0,8},{8,16},{16,24},{24,32},{32,40},{40,48},{48,56},{56,64},{64,7... | collective-permute-start | bytes 786440 | tf_op jit(solution)/shard_map/while/body/eval_jaxpr/ppermute | solution.py:13
  274.9 10.6 %collective-permute-start = (bf16[16,64,128]{2,1,0:T(8,128)(2,1)}, bf16[16,64,128]{2,1,0:T(8,128)(2,1)S(1)}, u32[]{:S(2)}, u32[]{:S(2)}) collective-permute-start(bf16[16,64,128]{2,1,0:T(8,128)(2,1)} %fusion.54), channel_id=1, source_target_pairs={{0,8},{8,16},{16,24},{24,32},{32,40},{40,48},{48,56},{56,64},{64,7... | collective-permute-start | bytes 786440 | tf_op jit(solution)/shard_map/while/body/eval_jaxpr/ppermute | solution.py:13
  288.4 10.6 %collective-permute-start = (bf16[16,64,128]{2,1,0:T(8,128)(2,1)}, bf16[16,64,128]{2,1,0:T(8,128)(2,1)S(1)}, u32[]{:S(2)}, u32[]{:S(2)}) collective-permute-start(bf16[16,64,128]{2,1,0:T(8,128)(2,1)} %fusion.54), channel_id=1, source_target_pairs={{0,8},{8,16},{16,24},{24,32},{32,40},{40,48},{48,56},{56,64},{64,7... | collective-permute-start | bytes 786440 | tf_op jit(solution)/shard_map/while/body/eval_jaxpr/ppermute | solution.py:13
  301.9 11.3 %collective-permute-start = (bf16[16,64,128]{2,1,0:T(8,128)(2,1)}, bf16[16,64,128]{2,1,0:T(8,128)(2,1)S(1)}, u32[]{:S(2)}, u32[]{:S(2)}) collective-permute-start(bf16[16,64,128]{2,1,0:T(8,128)(2,1)} %fusion.54), channel_id=1, source_target_pairs={{0,8},{8,16},{16,24},{24,32},{32,40},{40,48},{48,56},{56,64},{64,7... | collective-permute-start | bytes 786440 | tf_op jit(solution)/shard_map/while/body/eval_jaxpr/ppermute | solution.py:13
  316.1 12.5 %collective-permute-start = (bf16[16,64,128]{2,1,0:T(8,128)(2,1)}, bf16[16,64,128]{2,1,0:T(8,128)(2,1)S(1)}, u32[]{:S(2)}, u32[]{:S(2)}) collective-permute-start(bf16[16,64,128]{2,1,0:T(8,128)(2,1)} %fusion.54), channel_id=1, source_target_pairs={{0,8},{8,16},{16,24},{24,32},{32,40},{40,48},{48,56},{56,64},{64,7... | collective-permute-start | bytes 786440 | tf_op jit(solution)/shard_map/while/body/eval_jaxpr/ppermute | solution.py:13
  331.5 13.1 %collective-permute-start = (bf16[16,64,128]{2,1,0:T(8,128)(2,1)}, bf16[16,64,128]{2,1,0:T(8,128)(2,1)S(1)}, u32[]{:S(2)}, u32[]{:S(2)}) collective-permute-start(bf16[16,64,128]{2,1,0:T(8,128)(2,1)} %fusion.54), channel_id=1, source_target_pairs={{0,8},{8,16},{16,24},{24,32},{32,40},{40,48},{48,56},{56,64},{64,7... | collective-permute-start | bytes 786440 | tf_op jit(solution)/shard_map/while/body/eval_jaxpr/ppermute | solution.py:13
  347.6 12.3 %collective-permute-start = (bf16[16,64,128]{2,1,0:T(8,128)(2,1)}, bf16[16,64,128]{2,1,0:T(8,128)(2,1)S(1)}, u32[]{:S(2)}, u32[]{:S(2)}) collective-permute-start(bf16[16,64,128]{2,1,0:T(8,128)(2,1)} %fusion.54), channel_id=1, source_target_pairs={{0,8},{8,16},{16,24},{24,32},{32,40},{40,48},{48,56},{56,64},{64,7... | collective-permute-start | bytes 786440 | tf_op jit(solution)/shard_map/while/body/eval_jaxpr/ppermute | solution.py:13
  362.7 11.4 %collective-permute-start = (bf16[16,64,128]{2,1,0:T(8,128)(2,1)}, bf16[16,64,128]{2,1,0:T(8,128)(2,1)S(1)}, u32[]{:S(2)}, u32[]{:S(2)}) collective-permute-start(bf16[16,64,128]{2,1,0:T(8,128)(2,1)} %fusion.54), channel_id=1, source_target_pairs={{0,8},{8,16},{16,24},{24,32},{32,40},{40,48},{48,56},{56,64},{64,7... | collective-permute-start | bytes 786440 | tf_op jit(solution)/shard_map/while/body/eval_jaxpr/ppermute | solution.py:13
  404.0 13.2 %collective-permute-start = (bf16[16,64,128]{2,1,0:T(8,128)(2,1)}, bf16[16,64,128]{2,1,0:T(8,128)(2,1)S(1)}, u32[]{:S(2)}, u32[]{:S(2)}) collective-permute-start(bf16[16,64,128]{2,1,0:T(8,128)(2,1)} %fusion.54), channel_id=1, source_target_pairs={{0,8},{8,16},{16,24},{24,32},{32,40},{40,48},{48,56},{56,64},{64,7... | collective-permute-start | bytes 786440 | tf_op jit(solution)/shard_map/while/body/eval_jaxpr/ppermute | solution.py:13
  420.1 12.3 %collective-permute-start = (bf16[16,64,128]{2,1,0:T(8,128)(2,1)}, bf16[16,64,128]{2,1,0:T(8,128)(2,1)S(1)}, u32[]{:S(2)}, u32[]{:S(2)}) collective-permute-start(bf16[16,64,128]{2,1,0:T(8,128)(2,1)} %fusion.54), channel_id=1, source_target_pairs={{0,8},{8,16},{16,24},{24,32},{32,40},{40,48},{48,56},{56,64},{64,7... | collective-permute-start | bytes 786440 | tf_op jit(solution)/shard_map/while/body/eval_jaxpr/ppermute | solution.py:13
  435.3 11.6 %collective-permute-start = (bf16[16,64,128]{2,1,0:T(8,128)(2,1)}, bf16[16,64,128]{2,1,0:T(8,128)(2,1)S(1)}, u32[]{:S(2)}, u32[]{:S(2)}) collective-permute-start(bf16[16,64,128]{2,1,0:T(8,128)(2,1)} %fusion.54), channel_id=1, source_target_pairs={{0,8},{8,16},{16,24},{24,32},{32,40},{40,48},{48,56},{56,64},{64,7... | collective-permute-start | bytes 786440 | tf_op jit(solution)/shard_map/while/body/eval_jaxpr/ppermute | solution.py:13
  449.9 11.5 %collective-permute-start = (bf16[16,64,128]{2,1,0:T(8,128)(2,1)}, bf16[16,64,128]{2,1,0:T(8,128)(2,1)S(1)}, u32[]{:S(2)}, u32[]{:S(2)}) collective-permute-start(bf16[16,64,128]{2,1,0:T(8,128)(2,1)} %fusion.54), channel_id=1, source_target_pairs={{0,8},{8,16},{16,24},{24,32},{32,40},{40,48},{48,56},{56,64},{64,7... | collective-permute-start | bytes 786440 | tf_op jit(solution)/shard_map/while/body/eval_jaxpr/ppermute | solution.py:13
  470.2 12.5 %all-to-all-start = ((bf16[4,64,1024]{2,1,0:T(8,128)(2,1)}), bf16[4,64,1024]{2,1,0:T(8,128)(2,1)}, u32[]{:S(2)}, u32[]{:S(2)}) async-start(bf16[4,64,1024]{2,1,0:T(8,128)(2,1)} %copy.30), calls=%async_computation | async-start | bytes 1048576 | tf_op jit(solution)/shard_map/all_to_all | solution.py:57
  474.5 451.2 %reduce-scatter.2.cloned.1.call-start = ((), (), s32[]{:S(2)}) async-start(), calls=%async_computation.5 | async-start | bytes 8650752 | tf_op jit(solution)/shard_map/reduce_scatter | solution.py:96
  925.7 10.9 %all-to-all-start.3 = ((bf16[4,8,4096]{2,1,0:T(8,128)(2,1)}), bf16[4,8,4096]{2,1,0:T(8,128)(2,1)S(1)}, u32[]{:S(2)}, u32[]{:S(2)}) async-start(bf16[4,8,4096]{2,1,0:T(8,128)(2,1)} %bitcast.87), calls=%async_computation.4 | async-start | bytes 524288 | tf_op jit(solution)/shard_map/all_to_all | solution.py:103
  (14 other events, 1823.2 us)
Sparse Core Ops, SparseCore 0:
  699.6 226.1 reduce-scatter.1
